TPU v7x, 128 devices: a whole 4x4x4 slice. The times are simulated.
128 devices in a mesh: gx: 32 (over y, z_lo, x), gy: 4 (over z_hi, core).
Axes of the slice: x: 4, y: 4, z: 4 (z_hi: 2, z_lo: 2; z = z_hi * 2 + z_lo), core: 2. Of those that a mesh axis runs over, the one named last changes fastest.
Arguments:
- control: float32 [4, 4096, 1024], P(None, 'gx', 'gy'), may hold values from -6 to 6
- background_std: float32 [4, 4096, 1024], P(None, 'gx', 'gy'), may hold values from 0.5 to 2
- kappa_x: float32 [2, 4096, 1024], P(None, 'gx', 'gy'), may hold values from 0.02 to 0.24
- kappa_y: float32 [2, 4096, 1024], P(None, 'gx', 'gy'), may hold values from 0.02 to 0.24
- sea_mask: int32 [2, 4096, 1024], P(None, 'gx', 'gy'), may hold values 0 or 1
- obs_weights: bfloat16 [4096, 128, 256], P(('gx', 'gy')), may hold values from -0.375 to 0.375
- obs_values: float32 [4096, 128], P(('gx', 'gy')), may hold values from -6 to 6
- obs_rinv: float32 [4096, 128], P(('gx', 'gy')), may hold values from 0.5 to 2
- obs_tile: int32 [4096, 1], P(('gx', 'gy')), may hold values from 0 to 31; in each aligned block of 32 rows (0 to 31, 32 to 63, ...) at most 2 rows name the same one
- obs_offset: int32 [4096], P(('gx', 'gy')), may hold values from 0 to 511
Outputs:
- gradient: float32 [4, 4096, 1024], P(None, 'gx', 'gy')
- departures: float32 [4096, 128], P(('gx', 'gy'))
Inputs may be any that keep to these rules, and one draw needn't show every extreme that they name: `obs_tile`: among the blocks of one device at most 2 name the same tile column, and on at least one device exactly 2 blocks name the same tile column.
All inputs are finite; a program needn't handle non-finite values. No bound on the sum of `sea_mask` on one device may be relied on, other than what follows from the above.
Results may differ from a plain program's by a relative error of at most 0.00086.
Values may be sent and summed in bfloat16 or wider, within the bound.
A program may use at most 128 MiB of HBM per device.

v0:
```python
import jax
import jax.numpy as jnp
from jax import lax
from jax.sharding import PartitionSpec as P

VARS = 2
NSTEP = 8
SEG = 128


def with_halo(block, sides, width, periodic):
    for axis, dim in sides:
        count = lax.axis_size(axis)
        forward = [(i, i + 1) for i in range(count - 1)]
        if periodic:
            forward.append((count - 1, 0))
        backward = [(target, source) for source, target in forward]
        low = lax.ppermute(
            lax.slice_in_dim(block, block.shape[dim] - width, None, axis=dim), axis, forward
        )
        high = lax.ppermute(lax.slice_in_dim(block, 0, width, axis=dim), axis, backward)
        block = jnp.concatenate([low, block, high], axis=dim)
    return block


def tile_rims(planes_in, rim_cells):
    zonal_ext = with_halo(planes_in, (("gx", 1),), rim_cells, True)
    return with_halo(zonal_ext, (("gy", 2),), rim_cells, False)


def diffuse_once(padded, east_faces, north_faces):
    planes, extent_x, extent_y = padded.shape
    levels = east_faces.shape[0]
    cell_grid = padded.reshape(planes // levels, levels, extent_x, extent_y)
    center = cell_grid[:, :, 1:-1, 1:-1]
    east_flux = east_faces[:, 1:, 1:-1] * (cell_grid[:, :, 2:, 1:-1] - center)
    west_flux = east_faces[:, :-1, 1:-1] * (cell_grid[:, :, :-2, 1:-1] - center)
    north_flux = north_faces[:, 1:-1, 1:] * (cell_grid[:, :, 1:-1, 2:] - center)
    south_flux = north_faces[:, 1:-1, :-1] * (cell_grid[:, :, 1:-1, :-2] - center)
    result = center + east_flux + west_flux + north_flux + south_flux
    return result.reshape(planes, extent_x - 2, extent_y - 2)


def diffuse_local(planes_in, face_x, face_y, rim_cells):
    for sweep_index in range(NSTEP // rim_cells):
        padded = tile_rims(planes_in, rim_cells)
        padded = diffuse_once(padded, face_x, face_y)
        planes_in = padded
    return planes_in


def patch_table(state_low, levels):
    planes, rows_x, rows_y = state_low.shape
    split_cells = state_low.reshape(VARS, levels, rows_x, rows_y // SEG, SEG)
    return split_cells.transpose(1, 2, 3, 0, 4).reshape(
        levels * rows_x * (rows_y // SEG), VARS * SEG
    )


def table_field(patch_rows, levels, rows_x, rows_y):
    split_cells = patch_rows.reshape(levels, rows_x, rows_y // SEG, VARS, SEG)
    return split_cells.transpose(3, 0, 1, 2, 4).reshape(VARS * levels, rows_x, rows_y)


def slot_numbers(obs_tile, tile_count, capacity):
    target = obs_tile[:, 0]
    matches = (target[:, None] == jnp.arange(tile_count, dtype=jnp.int32)[None, :]).astype(
        jnp.int32
    )
    earlier = jnp.cumsum(matches, axis=0) - matches
    return target * capacity + jnp.sum(earlier * matches, axis=1)


def body(
    control,
    background_std,
    kappa_x,
    kappa_y,
    sea_mask,
    obs_weights,
    obs_values,
    obs_rinv,
    obs_tile,
    obs_offset,
):
    levels, rows_x, rows_y = kappa_x.shape
    tile_count = lax.axis_size("gx")
    blocks_here = obs_tile.shape[0]
    capacity = max(2, (2 * blocks_here + tile_count - 1) // tile_count)
    slot_total = tile_count * capacity
    patch_count = levels * rows_x * (rows_y // SEG)
    rim_cells = 1
    sea_float = sea_mask.astype(jnp.float32)
    coef_rims = tile_rims(jnp.concatenate([kappa_x, kappa_y, sea_float], axis=0), rim_cells)
    kappa_xpad = coef_rims[:levels]
    kappa_ypad = coef_rims[levels : 2 * levels]
    sea_pad = coef_rims[2 * levels :]
    face_x = kappa_xpad[:, :-1, :] * sea_pad[:, :-1, :] * sea_pad[:, 1:, :]
    face_y = kappa_ypad[:, :, :-1] * sea_pad[:, :, :-1] * sea_pad[:, :, 1:]
    sea_planes = jnp.concatenate([sea_float] * VARS, axis=0)
    state_field = background_std * diffuse_local(sea_planes * control, face_x, face_y, rim_cells)
    patch_rows = patch_table(state_field.astype(jnp.bfloat16), levels)
    slot_index = slot_numbers(obs_tile, tile_count, capacity)
    weights_send = (
        jnp.zeros((slot_total,) + obs_weights.shape[1:], jnp.bfloat16)
        .at[slot_index]
        .set(obs_weights)
    )
    meta_send = (
        jnp.zeros((slot_total, 2, obs_values.shape[1]), jnp.float32)
        .at[slot_index]
        .set(jnp.stack([obs_values, obs_rinv], axis=1))
    )
    offset_send = (
        jnp.zeros((slot_total,), jnp.float32).at[slot_index].set(obs_offset.astype(jnp.float32))
    )
    weights_got = lax.all_to_all(weights_send, "gx", split_axis=0, concat_axis=0, tiled=True)
    meta_got, offset_got = (
        lax.all_to_all(meta_send, "gx", split_axis=0, concat_axis=0, tiled=True),
        lax.all_to_all(offset_send, "gx", split_axis=0, concat_axis=0, tiled=True),
    )
    patch_index = offset_got.astype(jnp.int32)
    patches = jnp.take(patch_rows, patch_index, axis=0)
    equivalents = jnp.einsum("sop,sp->so", weights_got, patches, preferred_element_type=jnp.float32)
    slot_departures = meta_got[:, 1] * (equivalents - meta_got[:, 0])
    obs_terms = jnp.einsum(
        "sop,so->sp",
        weights_got,
        slot_departures.astype(jnp.bfloat16),
        preferred_element_type=jnp.float32,
    )
    forcing_rows = jax.ops.segment_sum(obs_terms, patch_index, num_segments=patch_count)
    returned = lax.all_to_all(slot_departures, "gx", split_axis=0, concat_axis=0, tiled=True)
    departures = jnp.take(returned, slot_index, axis=0)
    forcing = table_field(forcing_rows, levels, rows_x, rows_y)
    gradient = control + sea_planes * diffuse_local(
        background_std * forcing, face_x, face_y, rim_cells
    )
    return (gradient, departures)


def solution(mesh):
    in_specs = (
        P(None, "gx", "gy"),
        P(None, "gx", "gy"),
        P(None, "gx", "gy"),
        P(None, "gx", "gy"),
        P(None, "gx", "gy"),
        P(("gx", "gy"), None, None),
        P(("gx", "gy"), None),
        P(("gx", "gy"), None),
        P(("gx", "gy"), None),
        P(("gx", "gy")),
    )
    out_specs = (P(None, "gx", "gy"), P(("gx", "gy"), None))
    return jax.shard_map(body, mesh=mesh, in_specs=in_specs, out_specs=out_specs, check_vma=False)
```

profile of v0, /device:TPU:1, one launch (start us, length us, event | category | flops | bytes accessed | tf_op | source)
XLA Modules:
  0.0 528.4 jit_solution(15675291319786705807)
XLA Ops:
  16.0 6.6 %collective-permute-start.2 = (f32[4,130,1]{2,1,0:T(8,128)S(1)}, f32[4,130,1]{2,1,0:T(8,128)S(1)}, u32[]{:S(2)}, u32[]{:S(2)}) collective-permute-start(f32[4,130,1]{2,1,0:T(8,128)S(1)} %get-tuple-element.45), channel_id=1, source_target_pairs={{0,1},{1,2},{2,3},{4,5},{5,6},{6,7},{8,9},{9,10},{10,11},{12,13},{... | collective-permute-start | bytes 6248 | tf_op jit(solution)/shard_map/ppermute | solution.py:18
  54.9 6.6 %collective-permute-done.8 = f32[4,1,256]{1,2,0:T(8,128)S(1)} collective-permute-done((f32[4,1,256]{1,2,0:T(8,128)S(1)}, f32[4,1,256]{1,2,0:T(8,128)S(1)}, u32[]{:S(2)}, u32[]{:S(2)}) %collective-permute-start.8) | collective-permute-done | bytes 4128 | tf_op jit(solution)/shard_map/ppermute | solution.py:18
  78.8 8.9 %collective-permute-done.12 = f32[4,1,256]{1,2,0:T(8,128)S(1)} collective-permute-done((f32[4,1,256]{1,2,0:T(8,128)S(1)}, f32[4,1,256]{1,2,0:T(8,128)S(1)}, u32[]{:S(2)}, u32[]{:S(2)}) %collective-permute-start.12) | collective-permute-done | bytes 4128 | tf_op jit(solution)/shard_map/ppermute | solution.py:18
  98.1 6.0 %collective-permute-start.17 = (f32[4,1,256]{1,2,0:T(8,128)S(1)}, f32[4,1,256]{1,2,0:T(8,128)S(1)}, u32[]{:S(2)}, u32[]{:S(2)}) collective-permute-start(f32[4,1,256]{1,2,0:T(8,128)S(1)} %get-tuple-element.72), channel_id=1, source_target_pairs={{4,0},{8,4},{12,8},{16,12},{20,16},{24,20},{28,24},{32,28},{36,32}... | collective-permute-start | bytes 12296 | tf_op jit(solution)/shard_map/ppermute | solution.py:21
  104.3 8.9 %collective-permute-done.16 = f32[4,1,256]{1,2,0:T(8,128)S(1)} collective-permute-done((f32[4,1,256]{1,2,0:T(8,128)S(1)}, f32[4,1,256]{1,2,0:T(8,128)S(1)}, u32[]{:S(2)}, u32[]{:S(2)}) %collective-permute-start.16) | collective-permute-done | bytes 4128 | tf_op jit(solution)/shard_map/ppermute | solution.py:18
  119.0 7.7 %all-to-all-start = ((f32[32,2,1]{1,2,0:T(1,128)}), f32[32,2,1]{1,2,0:T(1,128)S(1)}, u32[]{:S(2)}, u32[]{:S(2)}) async-start(f32[32,2,1]{1,2,0:T(1,128)} %bitcast.3), calls=%async_computation | async-start | bytes 32768 | tf_op jit(solution)/shard_map/all_to_all | solution.py:120
  154.1 6.3 %scatter_fusion = bf16[64,128,256]{2,1,0:T(8,128)(2,1)} fusion(bf16[64,128,256]{2,1,0:T(8,128)(2,1)} %broadcast_in_dim.24, s32[32]{0:T(128)S(1)} %bitcast.147, bf16[32,128,256]{2,1,0:T(8,128)(2,1)} %param.15), kind=kCustom, calls=%fused_computation.3 | custom fusion | bytes 6291584 | tf_op jit(solution)/shard_map/scatter | solution.py:107
  160.4 7.4 %all-to-all-start.1 = ((bf16[64,128,256]{2,1,0:T(8,128)(2,1)}), bf16[64,128,256]{2,1,0:T(8,128)(2,1)}, u32[]{:S(2)}, u32[]{:S(2)}) async-start(bf16[64,128,256]{2,1,0:T(8,128)(2,1)} %scatter_fusion), calls=%async_computation.1 | async-start | bytes 8388608 | tf_op jit(solution)/shard_map/all_to_all | solution.py:117
  174.9 63.2 %collective-permute-done.24 = f32[4,1,256]{1,2,0:T(8,128)S(1)} collective-permute-done((f32[4,1,256]{1,2,0:T(8,128)S(1)}, f32[4,1,256]{1,2,0:T(8,128)S(1)}, u32[]{:S(2)}, u32[]{:S(2)}) %collective-permute-start.24) | collective-permute-done | bytes 4128 | tf_op jit(solution)/shard_map/ppermute | solution.py:18
  259.1 9.8 %collective-permute-done.28 = f32[4,1,256]{1,2,0:T(8,128)S(1)} collective-permute-done((f32[4,1,256]{1,2,0:T(8,128)S(1)}, f32[4,1,256]{1,2,0:T(8,128)S(1)}, u32[]{:S(2)}, u32[]{:S(2)}) %collective-permute-start.28) | collective-permute-done | bytes 4128 | tf_op jit(solution)/shard_map/ppermute | solution.py:18
  281.0 6.0 %collective-permute-start.33 = (f32[4,1,256]{1,2,0:T(8,128)S(1)}, f32[4,1,256]{1,2,0:T(8,128)S(1)}, u32[]{:S(2)}, u32[]{:S(2)}) collective-permute-start(f32[4,1,256]{1,2,0:T(8,128)S(1)} %get-tuple-element.64), channel_id=1, source_target_pairs={{4,0},{8,4},{12,8},{16,12},{20,16},{24,20},{28,24},{32,28},{36,32}... | collective-permute-start | bytes 12296 | tf_op jit(solution)/shard_map/ppermute | solution.py:21
  287.0 9.0 %collective-permute-done.32 = f32[4,1,256]{1,2,0:T(8,128)S(1)} collective-permute-done((f32[4,1,256]{1,2,0:T(8,128)S(1)}, f32[4,1,256]{1,2,0:T(8,128)S(1)}, u32[]{:S(2)}, u32[]{:S(2)}) %collective-permute-start.32) | collective-permute-done | bytes 4128 | tf_op jit(solution)/shard_map/ppermute | solution.py:18
  316.0 6.1 %collective-permute-start.37 = (f32[4,1,256]{1,2,0:T(8,128)S(1)}, f32[4,1,256]{1,2,0:T(8,128)S(1)}, u32[]{:S(2)}, u32[]{:S(2)}) collective-permute-start(f32[4,1,256]{1,2,0:T(8,128)S(1)} %get-tuple-element.62), channel_id=1, source_target_pairs={{4,0},{8,4},{12,8},{16,12},{20,16},{24,20},{28,24},{32,28},{36,32}... | collective-permute-start | bytes 12296 | tf_op jit(solution)/shard_map/ppermute | solution.py:21
  322.1 9.4 %collective-permute-done.36 = f32[4,1,256]{1,2,0:T(8,128)S(1)} collective-permute-done((f32[4,1,256]{1,2,0:T(8,128)S(1)}, f32[4,1,256]{1,2,0:T(8,128)S(1)}, u32[]{:S(2)}, u32[]{:S(2)}) %collective-permute-start.36) | collective-permute-done | bytes 4128 | tf_op jit(solution)/shard_map/ppermute | solution.py:18
  341.8 5.7 %collective-permute-start.41 = (f32[4,1,256]{1,2,0:T(8,128)S(1)}, f32[4,1,256]{1,2,0:T(8,128)S(1)}, u32[]{:S(2)}, u32[]{:S(2)}) collective-permute-start(f32[4,1,256]{1,2,0:T(8,128)S(1)} %get-tuple-element.60), channel_id=1, source_target_pairs={{4,0},{8,4},{12,8},{16,12},{20,16},{24,20},{28,24},{32,28},{36,32}... | collective-permute-start | bytes 12296 | tf_op jit(solution)/shard_map/ppermute | solution.py:21
  347.6 9.4 %collective-permute-done.40 = f32[4,1,256]{1,2,0:T(8,128)S(1)} collective-permute-done((f32[4,1,256]{1,2,0:T(8,128)S(1)}, f32[4,1,256]{1,2,0:T(8,128)S(1)}, u32[]{:S(2)}, u32[]{:S(2)}) %collective-permute-start.40) | collective-permute-done | bytes 4128 | tf_op jit(solution)/shard_map/ppermute | solution.py:18
  373.0 9.5 %collective-permute-done.44 = f32[4,1,256]{1,2,0:T(8,128)S(1)} collective-permute-done((f32[4,1,256]{1,2,0:T(8,128)S(1)}, f32[4,1,256]{1,2,0:T(8,128)S(1)}, u32[]{:S(2)}, u32[]{:S(2)}) %collective-permute-start.44) | collective-permute-done | bytes 4128 | tf_op jit(solution)/shard_map/ppermute | solution.py:18
  398.4 9.5 %collective-permute-done.48 = f32[4,1,256]{1,2,0:T(8,128)S(1)} collective-permute-done((f32[4,1,256]{1,2,0:T(8,128)S(1)}, f32[4,1,256]{1,2,0:T(8,128)S(1)}, u32[]{:S(2)}, u32[]{:S(2)}) %collective-permute-start.48) | collective-permute-done | bytes 4128 | tf_op jit(solution)/shard_map/ppermute | solution.py:18
  417.8 6.0 %collective-permute-start.53 = (f32[4,1,256]{1,2,0:T(8,128)S(1)}, f32[4,1,256]{1,2,0:T(8,128)S(1)}, u32[]{:S(2)}, u32[]{:S(2)}) collective-permute-start(f32[4,1,256]{1,2,0:T(8,128)S(1)} %get-tuple-element.54), channel_id=1, source_target_pairs={{4,0},{8,4},{12,8},{16,12},{20,16},{24,20},{28,24},{32,28},{36,32}... | collective-permute-start | bytes 12296 | tf_op jit(solution)/shard_map/ppermute | solution.py:21
  423.8 9.5 %collective-permute-done.52 = f32[4,1,256]{1,2,0:T(8,128)S(1)} collective-permute-done((f32[4,1,256]{1,2,0:T(8,128)S(1)}, f32[4,1,256]{1,2,0:T(8,128)S(1)}, u32[]{:S(2)}, u32[]{:S(2)}) %collective-permute-start.52) | collective-permute-done | bytes 4128 | tf_op jit(solution)/shard_map/ppermute | solution.py:18
  449.2 9.5 %collective-permute-done.56 = f32[4,1,256]{1,2,0:T(8,128)S(1)} collective-permute-done((f32[4,1,256]{1,2,0:T(8,128)S(1)}, f32[4,1,256]{1,2,0:T(8,128)S(1)}, u32[]{:S(2)}, u32[]{:S(2)}) %collective-permute-start.56) | collective-permute-done | bytes 4128 | tf_op jit(solution)/shard_map/ppermute | solution.py:18
  474.6 9.5 %collective-permute-done.60 = f32[4,1,256]{1,2,0:T(8,128)S(1)} collective-permute-done((f32[4,1,256]{1,2,0:T(8,128)S(1)}, f32[4,1,256]{1,2,0:T(8,128)S(1)}, u32[]{:S(2)}, u32[]{:S(2)}) %collective-permute-start.60) | collective-permute-done | bytes 4128 | tf_op jit(solution)/shard_map/ppermute | solution.py:18
  488.5 7.7 %all-to-all-start.3 = ((f32[32,2,128]{2,1,0:T(2,128)}), f32[32,2,128]{2,1,0:T(2,128)S(1)}, u32[]{:S(2)}, u32[]{:S(2)}) async-start(f32[32,2,128]{2,1,0:T(2,128)} %bitcast.50), calls=%async_computation.3 | async-start | bytes 65536 | tf_op jit(solution)/shard_map/all_to_all | solution.py:133
  504.7 12.0 %collective-permute-done.64 = f32[4,1,256]{1,2,0:T(8,128)S(1)} collective-permute-done((f32[4,1,256]{1,2,0:T(8,128)}, f32[4,1,256]{1,2,0:T(8,128)S(1)}, u32[]{:S(2)}, u32[]{:S(2)}) %collective-permute-start.64) | collective-permute-done | bytes 4128 | tf_op jit(solution)/shard_map/ppermute | solution.py:18
  (268 shorter events, 276.1 us)
Async XLA Ops:
  16.0 16.8 %collective-permute-start.2 = (f32[4,130,1]{2,1,0:T(8,128)S(1)}, f32[4,130,1]{2,1,0:T(8,128)S(1)}, u32[]{:S(2)}, u32[]{:S(2)}) collective-permute-start(f32[4,130,1]{2,1,0:T(8,128)S(1)} %get-tuple-element.45), channel_id=1, source_target_pairs={{0,1},{1,2},{2,3},{4,5},{5,6},{6,7},{8,9},{9,10},{10,11},{12,13},{... | collective-permute-start | bytes 6248 | tf_op jit(solution)/shard_map/ppermute | solution.py:18
  119.0 19.8 %all-to-all-start = ((f32[32,2,1]{1,2,0:T(1,128)}), f32[32,2,1]{1,2,0:T(1,128)S(1)}, u32[]{:S(2)}, u32[]{:S(2)}) async-start(f32[32,2,1]{1,2,0:T(1,128)} %bitcast.3), calls=%async_computation | async-start | bytes 32768 | tf_op jit(solution)/shard_map/all_to_all | solution.py:120
  128.9 18.2 %collective-permute-start.20 = (f32[4,1,256]{1,2,0:T(8,128)}, f32[4,1,256]{1,2,0:T(8,128)S(1)}, u32[]{:S(2)}, u32[]{:S(2)}) collective-permute-start(f32[4,1,256]{1,2,0:T(8,128)} %get-tuple-element.69), channel_id=1, source_target_pairs={{0,4},{4,8},{8,12},{12,16},{16,20},{20,24},{24,28},{28,32},{32,36}... | collective-permute-start | bytes 12296 | tf_op jit(solution)/shard_map/ppermute | solution.py:18
  130.1 17.0 %collective-permute-start.21 = (f32[4,1,256]{1,2,0:T(8,128)S(1)}, f32[4,1,256]{1,2,0:T(8,128)S(1)}, u32[]{:S(2)}, u32[]{:S(2)}) collective-permute-start(f32[4,1,256]{1,2,0:T(8,128)S(1)} %get-tuple-element.70), channel_id=1, source_target_pairs={{4,0},{8,4},{12,8},{16,12},{20,16},{24,20},{28,24},{32,28},{36,32}... | collective-permute-start | bytes 12296 | tf_op jit(solution)/shard_map/ppermute | solution.py:21
  138.8 21.6 %all-to-all-start.2 = ((f32[64,2,128]{2,1,0:T(2,128)}), f32[64,2,128]{2,1,0:T(2,128)S(1)}, u32[]{:S(2)}, u32[]{:S(2)}) async-start(f32[64,2,128]{2,1,0:T(2,128)} %scatter_fusion.1), calls=%async_computation.2 | async-start | bytes 131072 | tf_op jit(solution)/shard_map/all_to_all | solution.py:119
  147.2 20.5 %collective-permute-start.22 = (f32[4,130,1]{1,2,0:T(1,128)S(1)}, f32[4,130,1]{1,2,0:T(1,128)S(1)}, u32[]{:S(2)}, u32[]{:S(2)}) collective-permute-start(f32[4,130,1]{1,2,0:T(1,128)S(1)} %get-tuple-element.28), channel_id=1, source_target_pairs={{0,1},{1,2},{2,3},{4,5},{5,6},{6,7},{8,9},{9,10},{10,11},{12,13},{... | collective-permute-start | bytes 6248 | tf_op jit(solution)/shard_map/ppermute | solution.py:18
  149.2 18.6 %collective-permute-start.23 = (f32[4,130,1]{1,2,0:T(1,128)S(1)}, f32[4,130,1]{1,2,0:T(1,128)S(1)}, u32[]{:S(2)}, u32[]{:S(2)}) collective-permute-start(f32[4,130,1]{1,2,0:T(1,128)S(1)} %get-tuple-element.29), channel_id=1, source_target_pairs={{1,0},{2,1},{3,2},{5,4},{6,5},{7,6},{9,8},{10,9},{11,10},{13,12},{... | collective-permute-start | bytes 6248 | tf_op jit(solution)/shard_map/ppermute | solution.py:21
  160.4 146.9 %all-to-all-start.1 = ((bf16[64,128,256]{2,1,0:T(8,128)(2,1)}), bf16[64,128,256]{2,1,0:T(8,128)(2,1)}, u32[]{:S(2)}, u32[]{:S(2)}) async-start(bf16[64,128,256]{2,1,0:T(8,128)(2,1)} %scatter_fusion), calls=%async_computation.1 | async-start | bytes 8388608 | tf_op jit(solution)/shard_map/all_to_all | solution.py:117
  169.1 69.0 %collective-permute-start.24 = (f32[4,1,256]{1,2,0:T(8,128)S(1)}, f32[4,1,256]{1,2,0:T(8,128)S(1)}, u32[]{:S(2)}, u32[]{:S(2)}) collective-permute-start(f32[4,1,256]{1,2,0:T(8,128)S(1)} %get-tuple-element.67), channel_id=1, source_target_pairs={{0,4},{4,8},{8,12},{12,16},{16,20},{20,24},{24,28},{28,32},{32,36}... | collective-permute-start | bytes 12296 | tf_op jit(solution)/shard_map/ppermute | solution.py:18
  170.3 72.2 %collective-permute-start.25 = (f32[4,1,256]{1,2,0:T(8,128)S(1)}, f32[4,1,256]{1,2,0:T(8,128)S(1)}, u32[]{:S(2)}, u32[]{:S(2)}) collective-permute-start(f32[4,1,256]{1,2,0:T(8,128)S(1)} %get-tuple-element.68), channel_id=1, source_target_pairs={{4,0},{8,4},{12,8},{16,12},{20,16},{24,20},{28,24},{32,28},{36,32}... | collective-permute-start | bytes 12296 | tf_op jit(solution)/shard_map/ppermute | solution.py:21
  253.4 15.5 %collective-permute-start.28 = (f32[4,1,256]{1,2,0:T(8,128)S(1)}, f32[4,1,256]{1,2,0:T(8,128)S(1)}, u32[]{:S(2)}, u32[]{:S(2)}) collective-permute-start(f32[4,1,256]{1,2,0:T(8,128)S(1)} %get-tuple-element.65), channel_id=1, source_target_pairs={{0,4},{4,8},{8,12},{12,16},{16,20},{20,24},{24,28},{28,32},{32,36}... | collective-permute-start | bytes 12296 | tf_op jit(solution)/shard_map/ppermute | solution.py:18
  253.4 15.4 %collective-permute-start.29 = (f32[4,1,256]{1,2,0:T(8,128)S(1)}, f32[4,1,256]{1,2,0:T(8,128)S(1)}, u32[]{:S(2)}, u32[]{:S(2)}) collective-permute-start(f32[4,1,256]{1,2,0:T(8,128)S(1)} %get-tuple-element.66), channel_id=1, source_target_pairs={{4,0},{8,4},{12,8},{16,12},{20,16},{24,20},{28,24},{32,28},{36,32}... | collective-permute-start | bytes 12296 | tf_op jit(solution)/shard_map/ppermute | solution.py:21
  315.9 15.6 %collective-permute-start.36 = (f32[4,1,256]{1,2,0:T(8,128)S(1)}, f32[4,1,256]{1,2,0:T(8,128)S(1)}, u32[]{:S(2)}, u32[]{:S(2)}) collective-permute-start(f32[4,1,256]{1,2,0:T(8,128)S(1)} %get-tuple-element.61), channel_id=1, source_target_pairs={{0,4},{4,8},{8,12},{12,16},{16,20},{20,24},{24,28},{28,32},{32,36}... | collective-permute-start | bytes 12296 | tf_op jit(solution)/shard_map/ppermute | solution.py:18
  316.0 15.6 %collective-permute-start.37 = (f32[4,1,256]{1,2,0:T(8,128)S(1)}, f32[4,1,256]{1,2,0:T(8,128)S(1)}, u32[]{:S(2)}, u32[]{:S(2)}) collective-permute-start(f32[4,1,256]{1,2,0:T(8,128)S(1)} %get-tuple-element.62), channel_id=1, source_target_pairs={{4,0},{8,4},{12,8},{16,12},{20,16},{24,20},{28,24},{32,28},{36,32}... | collective-permute-start | bytes 12296 | tf_op jit(solution)/shard_map/ppermute | solution.py:21
  341.7 15.2 %collective-permute-start.40 = (f32[4,1,256]{1,2,0:T(8,128)S(1)}, f32[4,1,256]{1,2,0:T(8,128)S(1)}, u32[]{:S(2)}, u32[]{:S(2)}) collective-permute-start(f32[4,1,256]{1,2,0:T(8,128)S(1)} %get-tuple-element.59), channel_id=1, source_target_pairs={{0,4},{4,8},{8,12},{12,16},{16,20},{20,24},{24,28},{28,32},{32,36}... | collective-permute-start | bytes 12296 | tf_op jit(solution)/shard_map/ppermute | solution.py:18
  367.1 15.3 %collective-permute-start.44 = (f32[4,1,256]{1,2,0:T(8,128)S(1)}, f32[4,1,256]{1,2,0:T(8,128)S(1)}, u32[]{:S(2)}, u32[]{:S(2)}) collective-permute-start(f32[4,1,256]{1,2,0:T(8,128)S(1)} %get-tuple-element.57), channel_id=1, source_target_pairs={{0,4},{4,8},{8,12},{12,16},{16,20},{20,24},{24,28},{28,32},{32,36}... | collective-permute-start | bytes 12296 | tf_op jit(solution)/shard_map/ppermute | solution.py:18
  392.6 15.2 %collective-permute-start.48 = (f32[4,1,256]{1,2,0:T(8,128)S(1)}, f32[4,1,256]{1,2,0:T(8,128)S(1)}, u32[]{:S(2)}, u32[]{:S(2)}) collective-permute-start(f32[4,1,256]{1,2,0:T(8,128)S(1)} %get-tuple-element.55), channel_id=1, source_target_pairs={{0,4},{4,8},{8,12},{12,16},{16,20},{20,24},{24,28},{28,32},{32,36}... | collective-permute-start | bytes 12296 | tf_op jit(solution)/shard_map/ppermute | solution.py:18
  417.7 15.5 %collective-permute-start.52 = (f32[4,1,256]{1,2,0:T(8,128)S(1)}, f32[4,1,256]{1,2,0:T(8,128)S(1)}, u32[]{:S(2)}, u32[]{:S(2)}) collective-permute-start(f32[4,1,256]{1,2,0:T(8,128)S(1)} %get-tuple-element.53), channel_id=1, source_target_pairs={{0,4},{4,8},{8,12},{12,16},{16,20},{20,24},{24,28},{28,32},{32,36}... | collective-permute-start | bytes 12296 | tf_op jit(solution)/shard_map/ppermute | solution.py:18
  417.8 15.5 %collective-permute-start.53 = (f32[4,1,256]{1,2,0:T(8,128)S(1)}, f32[4,1,256]{1,2,0:T(8,128)S(1)}, u32[]{:S(2)}, u32[]{:S(2)}) collective-permute-start(f32[4,1,256]{1,2,0:T(8,128)S(1)} %get-tuple-element.54), channel_id=1, source_target_pairs={{4,0},{8,4},{12,8},{16,12},{20,16},{24,20},{28,24},{32,28},{36,32}... | collective-permute-start | bytes 12296 | tf_op jit(solution)/shard_map/ppermute | solution.py:21
  443.4 15.2 %collective-permute-start.56 = (f32[4,1,256]{1,2,0:T(8,128)S(1)}, f32[4,1,256]{1,2,0:T(8,128)S(1)}, u32[]{:S(2)}, u32[]{:S(2)}) collective-permute-start(f32[4,1,256]{1,2,0:T(8,128)S(1)} %get-tuple-element.51), channel_id=1, source_target_pairs={{0,4},{4,8},{8,12},{12,16},{16,20},{20,24},{24,28},{28,32},{32,36}... | collective-permute-start | bytes 12296 | tf_op jit(solution)/shard_map/ppermute | solution.py:18
  468.9 15.2 %collective-permute-start.60 = (f32[4,1,256]{1,2,0:T(8,128)S(1)}, f32[4,1,256]{1,2,0:T(8,128)S(1)}, u32[]{:S(2)}, u32[]{:S(2)}) collective-permute-start(f32[4,1,256]{1,2,0:T(8,128)S(1)} %get-tuple-element.49), channel_id=1, source_target_pairs={{0,4},{4,8},{8,12},{12,16},{16,20},{20,24},{24,28},{28,32},{32,36}... | collective-permute-start | bytes 12296 | tf_op jit(solution)/shard_map/ppermute | solution.py:18
  488.5 15.6 %all-to-all-start.3 = ((f32[32,2,128]{2,1,0:T(2,128)}), f32[32,2,128]{2,1,0:T(2,128)S(1)}, u32[]{:S(2)}, u32[]{:S(2)}) async-start(f32[32,2,128]{2,1,0:T(2,128)} %bitcast.50), calls=%async_computation.3 | async-start | bytes 65536 | tf_op jit(solution)/shard_map/all_to_all | solution.py:133
  498.4 18.2 %collective-permute-start.64 = (f32[4,1,256]{1,2,0:T(8,128)}, f32[4,1,256]{1,2,0:T(8,128)S(1)}, u32[]{:S(2)}, u32[]{:S(2)}) collective-permute-start(f32[4,1,256]{1,2,0:T(8,128)} %get-tuple-element.47), channel_id=1, source_target_pairs={{0,4},{4,8},{8,12},{12,16},{16,20},{20,24},{24,28},{28,32},{32,36}... | collective-permute-start | bytes 12296 | tf_op jit(solution)/shard_map/ppermute | solution.py:18
  499.6 17.0 %collective-permute-start.65 = (f32[4,1,256]{1,2,0:T(8,128)S(1)}, f32[4,1,256]{1,2,0:T(8,128)S(1)}, u32[]{:S(2)}, u32[]{:S(2)}) collective-permute-start(f32[4,1,256]{1,2,0:T(8,128)S(1)} %get-tuple-element.48), channel_id=1, source_target_pairs={{4,0},{8,4},{12,8},{16,12},{20,16},{24,20},{28,24},{32,28},{36,32}... | collective-permute-start | bytes 12296 | tf_op jit(solution)/shard_map/ppermute | solution.py:21
  (59 other events, 612.4 us)
where the time goes:
time: 538 us; the launch traced here: 528 us
  waiting for transfers between devices  249 us (46%)
  starting transfers between devices  209 us (39%)
  other arithmetic  31 us (6%)
  local copies, waits for them, and re-layouts  30.6 us (6%)
  matrix products  6.19 us (1%)
    ppermute x34, waiting for transfers between devices, with_halo(): lax.ppermute(lax.slice_in_dim(block, block.shape[dim] - width, None, axis...  189 us
    ppermute x34, starting transfers between devices, with_halo(): lax.ppermute(lax.slice_in_dim(block, 0, width, axis=dim), axis, backward)  134 us
    ppermute x34, waiting for transfers between devices, with_halo(): lax.ppermute(lax.slice_in_dim(block, 0, width, axis=dim), axis, backward)  60.3 us
    ppermute x34, starting transfers between devices, with_halo(): lax.ppermute(lax.slice_in_dim(block, block.shape[dim] - width, None, axis...  48.7 us
    concatenate x19, other arithmetic, with_halo(): block = jnp.concatenate([low, block, high], axis=dim)  11.6 us
  transfers between devices with their start and end apart: 72, of which 29 were waited for; matrix products, arithmetic and copies ran while one was open for 6% of the time, Pallas kernels for 0%

commit v1 on v0

v1 whole, which is shorter than its diff:
```python
import functools

import jax
import jax.numpy as jnp
from jax import lax
from jax.experimental import pallas as pl
from jax.experimental.pallas import tpu as pltpu
from jax.sharding import PartitionSpec as P

VARS = 2
NSTEP = 8
LANES = 128
RIM = 8
CAP = 2
TOP = 2 * RIM
CHUNK = 16
MESH = pl.DeviceIdType.MESH
F32 = jnp.float32
BF16 = jnp.bfloat16


def lane_iota(shape):
    return lax.broadcasted_iota(jnp.int32, shape, len(shape) - 1)


def row_iota(shape):
    return lax.broadcasted_iota(jnp.int32, shape, len(shape) - 2)


def north_of(tiles, last_lane):
    rolled = [pltpu.roll(tile, LANES - 1, 1) for tile in tiles]
    count = len(tiles)
    return [jnp.where(last_lane, rolled[(t + 1) % count], rolled[t]) for t in range(count)]


def south_of(tiles, first_lane):
    rolled = [pltpu.roll(tile, 1, 1) for tile in tiles]
    count = len(tiles)
    return [jnp.where(first_lane, rolled[(t - 1) % count], rolled[t]) for t in range(count)]


def diffuse_step(src, dst, fx, fy, levels, rows):
    ntile = src.shape[1]
    first_lane = lane_iota((CHUNK, LANES)) == 0
    last_lane = lane_iota((CHUNK, LANES)) == LANES - 1
    for level in range(levels):
        for base in range(RIM, RIM + rows + 2 * RIM, CHUNK):
            here, above, below = (
                pl.ds(base, CHUNK),
                pl.ds(base + 1, CHUNK),
                pl.ds(base - 1, CHUNK),
            )
            east = [fx[level, t, here, :] for t in range(ntile)]
            west = [fx[level, t, below, :] for t in range(ntile)]
            north = [fy[level, t, here, :] for t in range(ntile)]
            for var in range(VARS):
                plane = var * levels + level
                center = [src[plane, t, here, :] for t in range(ntile)]
                up = north_of(center, last_lane)
                flux = [north[t] * (up[t] - center[t]) for t in range(ntile)]
                back = south_of(flux, first_lane)
                for t in range(ntile):
                    cell = center[t]
                    dst[plane, t, here, :] = (
                        cell
                        + east[t] * (src[plane, t, above, :] - cell)
                        + west[t] * (src[plane, t, below, :] - cell)
                        + flux[t]
                        - back[t]
                    )


def diffuse(first, second, fx, fy, levels, rows):
    def twice(_, carry):
        diffuse_step(first, second, fx, fy, levels, rows)
        diffuse_step(second, first, fx, fy, levels, rows)
        return carry

    lax.fori_loop(0, NSTEP // 2, twice, 0)


def split_three(value):
    high = value.astype(BF16)
    rest = value - high.astype(F32)
    middle = rest.astype(BF16)
    low = (rest - middle.astype(F32)).astype(BF16)
    return high, middle, low


def exact_dot(ones, value):
    width = value.shape[1]
    parts = jnp.concatenate(split_three(value), axis=1)
    sums = jnp.dot(ones, parts, preferred_element_type=F32)
    return sums[:, :width] + sums[:, width : 2 * width] + sums[:, 2 * width :]


def kernel(
    n_x,
    n_y,
    control,
    background_std,
    kappa_x,
    kappa_y,
    sea_mask,
    obs_weights,
    obs_values,
    obs_rinv,
    tile_row,
    offset_row,
    gradient,
    departures,
    xin,
    sea_in,
    std,
    weights,
    sea,
    fx,
    fy,
    field_a,
    field_b,
    field_c,
    strip_out,
    strip_in,
    strip_out2,
    strip_in2,
    index_out,
    index_in,
    patch_out,
    patch_in,
    term_out,
    term_in,
    terms,
    out_tile,
    load_sem,
    x_send,
    x_recv,
    y_send,
    y_recv,
    x2_send,
    x2_recv,
    y2_send,
    y2_recv,
    all_send,
    all_recv,
):
    planes, rows, cols = control.shape
    levels = planes // VARS
    blocks = obs_values.shape[0]
    segs = cols // LANES
    ix, jy = lax.axis_index("gx"), lax.axis_index("gy")
    east, west = lax.rem(ix + 1, n_x), lax.rem(ix + n_x - 1, n_x)
    north, south = lax.rem(jy + 1, n_y), lax.rem(jy + n_y - 1, n_y)
    own = pl.ds(TOP, rows)
    low_rim, high_rim = pl.ds(RIM, RIM), pl.ds(TOP + rows, RIM)
    low_edge, high_edge = pl.ds(TOP, RIM), pl.ds(TOP + rows - RIM, RIM)
    ext = pl.ds(RIM, rows + 2 * RIM)
    ext_rows = rows + 2 * RIM
    height = rows + 4 * RIM

    barrier = pltpu.get_barrier_semaphore()

    def greet(step, carry):
        pl.semaphore_signal(
            barrier, inc=1, device_id=(lax.rem(ix + step, n_x), jy), device_id_type=MESH
        )
        return carry

    lax.fori_loop(1, n_x, greet, 0)
    for other_y in (north, south):
        for other_x in (west, ix, east):
            pl.semaphore_signal(
                barrier, inc=1, device_id=(other_x, other_y), device_id_type=MESH
            )

    loads = []

    def load(source, target):
        copy = pltpu.make_async_copy(source, target, load_sem.at[len(loads)])
        copy.start()
        loads.append(copy)

    for t in range(segs):
        span = pl.ds(t * LANES, LANES)
        load(sea_mask.at[:, :, span], sea_in.at[:, t, own, :])
        load(kappa_x.at[:, :, span], xin.at[pl.ds(planes, levels), t, own, :])
        load(kappa_y.at[:, :, span], xin.at[pl.ds(planes + levels, levels), t, own, :])
        load(control.at[:, :, span], xin.at[pl.ds(0, planes), t, own, :])
    late = len(loads)
    for t in range(segs):
        load(background_std.at[:, :, pl.ds(t * LANES, LANES)], std.at[:, t, :, :])
    load(obs_weights, weights)

    edge = jnp.zeros((RIM, LANES), F32)
    for ref in (field_a, field_b, field_c):
        for plane in range(planes):
            for t in range(segs + 1):
                ref[plane, t, pl.ds(0, RIM), :] = edge
                ref[plane, t, pl.ds(height - RIM, RIM), :] = edge
    for level in range(levels):
        for t in range(segs + 1):
            fx[level, t, pl.ds(0, RIM), :] = edge
            sea[level, t, pl.ds(height - RIM, RIM), :] = edge

    row = tile_row[...].astype(F32)
    pair = (blocks, blocks)
    diagonal = lane_iota(pair) == row_iota(pair)
    col = jnp.sum(jnp.where(diagonal, row, 0.0), axis=1, keepdims=True)
    same = col == row
    rank_col = jnp.max(
        jnp.where(same & (lane_iota(pair) < row_iota(pair)), 1.0, 0.0), axis=1, keepdims=True
    )
    rank_row = jnp.max(
        jnp.where(same & (row_iota(pair) < lane_iota(pair)), 1.0, 0.0), axis=0, keepdims=True
    )
    slots = CAP * n_x
    slot_lane = lane_iota((blocks, slots))
    late_lane = slot_lane >= n_x
    block_slot = jnp.where(
        (jnp.where(late_lane, slot_lane - n_x, slot_lane).astype(F32) == col)
        & (jnp.where(late_lane, 1.0, 0.0) == rank_col),
        1.0,
        0.0,
    ).astype(BF16)
    slot_row = row_iota((slots, blocks))
    late_row = slot_row >= n_x
    slot_block = jnp.where(
        (jnp.where(late_row, slot_row - n_x, slot_row).astype(F32) == row)
        & (jnp.where(late_row, 1.0, 0.0) == rank_row),
        1.0,
        0.0,
    )
    wanted = (
        jnp.sum(slot_block * (offset_row[...].astype(F32) + 1.0), axis=1, keepdims=True) - 1.0
    )
    wanted = jnp.broadcast_to(wanted, (slots, LANES))
    for c in range(CAP):
        index_out[:, 0, pl.ds(c * LANES, LANES)] = wanted[c * n_x : (c + 1) * n_x]

    for copy in loads[:late]:
        copy.wait()
    strip_lane = lane_iota((rows, LANES))
    for side, t in ((0, 0), (1, segs - 1)):
        strip = jnp.zeros((rows, LANES), F32)
        for index in range(planes + 2 * levels):
            level = index % levels
            value = jnp.where(sea_in[level, t, own, :] > 0, xin[index, t, own, :], 0.0)
            shift = (index * RIM + side * RIM) % LANES
            if shift:
                value = pltpu.roll(value, shift, 1)
            here = (strip_lane >= index * RIM) & (strip_lane < (index + 1) * RIM)
            strip = jnp.where(here, value, strip)
        strip_out[side] = strip

    pl.semaphore_wait(barrier, n_x - 1 + 6)

    def send(source, target, sems, number, device):
        copy = pltpu.make_async_remote_copy(
            source,
            target,
            sems[0].at[number],
            sems[1].at[number],
            device_id=device,
            device_id_type=MESH,
        )
        copy.start()
        return copy

    def send_x(refs, sems):
        return [
            send(
                ref.at[:, pl.ds(0, segs), edge_rows, :],
                ref.at[:, pl.ds(0, segs), rim_rows, :],
                sems,
                2 * number + side,
                (other, jy),
            )
            for number, ref in enumerate(refs)
            for side, edge_rows, rim_rows, other in (
                (0, low_edge, high_rim, west),
                (1, high_edge, low_rim, east),
            )
        ]

    def send_y(source, target, sems):
        copies = []
        for side, other_y in ((0, south), (1, north)):
            for number, from_rows, to_rows, other_x in (
                (0, pl.ds(0, rows), own, ix),
                (1, pl.ds(0, RIM), high_rim, west),
                (2, pl.ds(rows - RIM, RIM), low_rim, east),
            ):
                copies.append(
                    send(
                        source.at[side, from_rows, :],
                        target.at[1 - side, to_rows, :],
                        sems,
                        3 * side + number,
                        (other_x, other_y),
                    )
                )
        return copies

    def send_all(source, target, number):
        def one(step, carry):
            other = lax.rem(ix + step, n_x)
            pltpu.make_async_remote_copy(
                source.at[other],
                target.at[ix],
                all_send.at[number],
                all_recv.at[number],
                device_id=(other, jy),
                device_id_type=MESH,
            ).start()
            return carry

        lax.fori_loop(1, n_x, one, 0)
        target[pl.ds(ix, 1)] = source[pl.ds(ix, 1)]
        return pltpu.make_async_remote_copy(
            source.at[pl.ds(0, n_x - 1)],
            target.at[pl.ds(0, n_x - 1)],
            all_send.at[number],
            all_recv.at[number],
            device_id=(east, jy),
            device_id_type=MESH,
        )

    sent_y = send_y(strip_out, strip_in, (y_send, y_recv))
    sent_x = send_x((xin, sea_in), (x_send, x_recv))
    sent_index = send_all(index_out, index_in, 0)

    for copy in sent_x:
        copy.wait()
    for level in range(levels):
        for t in range(segs):
            wet = sea_in[level, t, ext, :] > 0
            sea[level, t, ext, :] = jnp.where(wet, 1.0, 0.0)
            fx[level, t, ext, :] = jnp.where(wet, xin[planes + level, t, ext, :], 0.0)
            fy[level, t, ext, :] = jnp.where(wet, xin[planes + levels + level, t, ext, :], 0.0)
            for var in range(VARS):
                plane = var * levels + level
                field_a[plane, t, ext, :] = jnp.where(wet, xin[plane, t, ext, :], 0.0)
    for copy in sent_y:
        copy.wait()
    ext_lane = lane_iota((ext_rows, LANES))
    from_low = (ext_lane >= LANES - RIM) & (jy > 0)
    from_high = (ext_lane < RIM) & (jy < n_y - 1)

    def unpack(strips, index):
        low = pltpu.roll(strips[0, ext, :], (LANES - RIM - index * RIM) % LANES, 1)
        high = strips[1, ext, :]
        if index:
            high = pltpu.roll(high, LANES - index * RIM, 1)
        return jnp.where(from_high, high, jnp.where(from_low, low, 0.0))

    for plane in range(planes):
        field_a[plane, segs, ext, :] = unpack(strip_in, plane)
    for level in range(levels):
        face = unpack(strip_in, planes + level)
        fx[level, segs, ext, :] = face
        sea[level, segs, ext, :] = jnp.where(face > 0.0, 1.0, 0.0)
        fy[level, segs, ext, :] = unpack(strip_in, planes + levels + level)
    last_lane = ext_lane == LANES - 1
    for level in range(levels):
        wet_north = north_of([sea[level, t, ext, :] for t in range(segs + 1)], last_lane)
        for t in range(segs + 1):
            fx[level, t, ext, :] = (
                fx[level, t, ext, :] * sea[level, t, pl.ds(RIM + 1, ext_rows), :]
            )
            fy[level, t, ext, :] = fy[level, t, ext, :] * wet_north[t]

    diffuse(field_a, field_b, fx, fy, levels, rows)

    for copy in loads[late:]:
        copy.wait()
    sent_index.wait()
    asked = jnp.concatenate(
        [index_in[:, 0, pl.ds(c * LANES, LANES)] for c in range(CAP)], axis=0
    )
    number = lane_iota((slots, LANES)) * segs
    if rows < LANES:
        number = jnp.where(number < rows * segs, number, -2)
    hits = jnp.concatenate(
        [
            jnp.where(asked == (number + (level * rows * segs + s)).astype(F32), 1.0, 0.0)
            for level in range(levels)
            for s in range(segs)
        ],
        axis=1,
    ).astype(BF16)
    table = jnp.concatenate(
        [
            jnp.concatenate(
                [
                    (std[v * levels + level, s] * field_a[v * levels + level, s, own, :]).astype(
                        BF16
                    )
                    for v in range(VARS)
                ],
                axis=1,
            )
            for level in range(levels)
            for s in range(segs)
        ],
        axis=0,
    )
    patch_width = VARS * LANES
    picked = jnp.dot(hits, table, preferred_element_type=F32)
    for c in range(CAP):
        patch_out[:, 0, pl.ds(c * patch_width, patch_width)] = picked[c * n_x : (c + 1) * n_x]
    sent_patch = send_all(patch_out, patch_in, 1)
    sent_patch.wait()
    arrived = jnp.concatenate(
        [patch_in[:, 0, pl.ds(c * patch_width, patch_width)] for c in range(CAP)], axis=0
    ).astype(BF16)
    patches = jnp.dot(block_slot, arrived, preferred_element_type=F32).astype(BF16)

    nobs = obs_values.shape[1]
    obs_lane = lane_iota((nobs, LANES))
    padded = jnp.concatenate(
        [patches, jnp.zeros((LANES - blocks, patch_width), BF16)], axis=0
    )

    def one_equivalent(b, total):
        product = lax.dot_general(
            weights[b], padded, (((1,), (1,)), ((), ())), preferred_element_type=F32
        )
        return jnp.where(obs_lane == b, product, total)

    equivalents = lax.fori_loop(0, blocks, one_equivalent, jnp.zeros((nobs, LANES), F32))
    departed = obs_rinv[...] * (equivalents.T[:blocks] - obs_values[...])
    departures[...] = departed
    low = departed.astype(BF16).astype(F32)
    low_cols = jnp.concatenate([low, jnp.zeros((LANES - blocks, nobs), F32)], axis=0).T

    def one_term(b, carry):
        column = jnp.sum(jnp.where(obs_lane == b, low_cols, 0.0), axis=1, keepdims=True)
        terms[pl.ds(b, 1), :] = jnp.sum(weights[b].astype(F32) * column, axis=0, keepdims=True)
        return carry

    lax.fori_loop(0, blocks, one_term, 0)
    outgoing = exact_dot(slot_block.astype(BF16), terms[...])
    for c in range(CAP):
        term_out[:, 0, pl.ds(c * patch_width, patch_width)] = outgoing[c * n_x : (c + 1) * n_x]
    sent_term = send_all(term_out, term_in, 2)
    sent_term.wait()
    returned = jnp.concatenate(
        [term_in[:, 0, pl.ds(c * patch_width, patch_width)] for c in range(CAP)], axis=0
    )

    asked_cols = jnp.concatenate(
        [asked, jnp.full((LANES - slots, LANES), -1.0, F32)], axis=0
    ).T[:rows, :slots]
    cell = row_iota((rows, slots)) * segs
    spread = jnp.concatenate(
        [
            jnp.where(asked_cols == (cell + (level * rows * segs + s)).astype(F32), 1.0, 0.0)
            for level in range(levels)
            for s in range(segs)
        ],
        axis=0,
    ).astype(BF16)
    forcing = exact_dot(spread, returned)
    for level in range(levels):
        for s in range(segs):
            start = (level * segs + s) * rows
            for v in range(VARS):
                plane = v * levels + level
                field_c[plane, s, own, :] = (
                    std[plane, s]
                    * forcing[start : start + rows, v * LANES : (v + 1) * LANES]
                )
    for side, t in ((0, 0), (1, segs - 1)):
        strip = jnp.zeros((rows, LANES), F32)
        for plane in range(planes):
            value = field_c[plane, t, own, :]
            shift = (plane * RIM + side * RIM) % LANES
            if shift:
                value = pltpu.roll(value, shift, 1)
            here = (strip_lane >= plane * RIM) & (strip_lane < (plane + 1) * RIM)
            strip = jnp.where(here, value, strip)
        strip_out2[side] = strip
    sent_x2 = send_x((field_c,), (x2_send, x2_recv))
    sent_y2 = send_y(strip_out2, strip_in2, (y2_send, y2_recv))
    for copy in sent_x2 + sent_y2:
        copy.wait()
    for plane in range(planes):
        field_c[plane, segs, ext, :] = unpack(strip_in2, plane)

    diffuse(field_c, field_b, fx, fy, levels, rows)

    stores = []
    for s in range(segs):
        for plane in range(planes):
            out_tile[plane, s] = (
                xin[plane, s, own, :]
                + sea[plane % levels, s, own, :] * field_c[plane, s, own, :]
            )
        copy = pltpu.make_async_copy(
            out_tile.at[:, s, :, :],
            gradient.at[:, :, pl.ds(s * LANES, LANES)],
            load_sem.at[s],
        )
        copy.start()
        stores.append(copy)
    for copy in stores:
        copy.wait()


def body(
    n_x,
    n_y,
    control,
    background_std,
    kappa_x,
    kappa_y,
    sea_mask,
    obs_weights,
    obs_values,
    obs_rinv,
    obs_tile,
    obs_offset,
):
    planes, rows, cols = control.shape
    levels = kappa_x.shape[0]
    blocks, nobs, width = obs_weights.shape
    segs = cols // LANES
    height = rows + 4 * RIM
    inputs = planes + 2 * levels
    hbm = pl.BlockSpec(memory_space=pl.ANY)
    vmem = pl.BlockSpec(memory_space=pltpu.VMEM)
    dma = pltpu.SemaphoreType.DMA
    field = pltpu.VMEM((planes, segs + 1, height, LANES), F32)
    face = pltpu.VMEM((levels, segs + 1, height, LANES), F32)
    return pl.pallas_call(
        functools.partial(kernel, n_x, n_y),
        out_shape=(
            jax.ShapeDtypeStruct(control.shape, F32),
            jax.ShapeDtypeStruct(obs_values.shape, F32),
        ),
        in_specs=[hbm] * 6 + [vmem] * 4,
        out_specs=(hbm, vmem),
        scratch_shapes=[
            pltpu.VMEM((inputs, segs, height, LANES), F32),
            pltpu.VMEM((levels, segs, height, LANES), jnp.int32),
            pltpu.VMEM((planes, segs, rows, LANES), F32),
            pltpu.VMEM((blocks, nobs, width), BF16),
            face,
            face,
            face,
            field,
            field,
            field,
            pltpu.VMEM((2, rows, LANES), F32),
            pltpu.VMEM((2, height, LANES), F32),
            pltpu.VMEM((2, rows, LANES), F32),
            pltpu.VMEM((2, height, LANES), F32),
            pltpu.VMEM((n_x, 1, CAP * LANES), F32),
            pltpu.VMEM((n_x, 1, CAP * LANES), F32),
            pltpu.VMEM((n_x, 1, CAP * width), F32),
            pltpu.VMEM((n_x, 1, CAP * width), F32),
            pltpu.VMEM((n_x, 1, CAP * width), F32),
            pltpu.VMEM((n_x, 1, CAP * width), F32),
            pltpu.VMEM((blocks, width), F32),
            pltpu.VMEM((planes, segs, rows, LANES), F32),
            dma((5 * segs + 1,)),
            dma((4,)),
            dma((4,)),
            dma((6,)),
            dma((6,)),
            dma((2,)),
            dma((2,)),
            dma((6,)),
            dma((6,)),
            dma((3,)),
            dma((3,)),
        ],
        compiler_params=pltpu.CompilerParams(
            collective_id=0, has_side_effects=True, vmem_limit_bytes=66_000_000
        ),
        name="variational_gradient",
    )(
        control,
        background_std,
        kappa_x,
        kappa_y,
        sea_mask,
        obs_weights,
        obs_values,
        obs_rinv,
        obs_tile.reshape(1, blocks),
        obs_offset.reshape(1, blocks),
    )


def solution(mesh):
    grid = P(None, "gx", "gy")
    holder = ("gx", "gy")
    in_specs = (
        grid,
        grid,
        grid,
        grid,
        grid,
        P(holder, None, None),
        P(holder, None),
        P(holder, None),
        P(holder, None),
        P(holder),
    )
    return jax.shard_map(
        functools.partial(body, mesh.shape["gx"], mesh.shape["gy"]),
        mesh=mesh,
        in_specs=in_specs,
        out_specs=(grid, P(holder, None)),
        check_vma=False,
    )
```

time: 538 us -> 88.5 us (0.16); the launches traced: 528 us -> 88.3 us
  waiting for transfers between devices: 249 us -> 0 us
  starting transfers between devices: 209 us -> 0 us
  Pallas kernels: 0 us -> 84.4 us
  other arithmetic: 31 us -> 0 us
  local copies, waits for them, and re-layouts: 30.6 us -> 3.19 us
  matrix products: 6.19 us -> 0 us
    ppermute x68 -> x0, waiting for transfers between devices: 249 us -> none  [the longest x34 189 us: with_halo(): lax.ppermute(lax.slice_in_dim(block, block.shape[dim] - width, None, axis...]
    ppermute x68 -> x0, starting transfers between devices: 183 us -> none  [the longest x34 134 us: with_halo(): lax.ppermute(lax.slice_in_dim(block, 0, width, axis=dim), axis, backward)]
    pallas_call x0 -> x1, Pallas kernels: none -> 84.4 us  [body(): pl.pallas_call(functools.partial(kernel, n_x, n_y), out_shape=(jax.ShapeD...]
    all_to_all x4 -> x0, starting transfers between devices: 26.7 us -> none  [the longest x1 7.72 us: body(): lax.all_to_all(slot_departures, 'gx', split_axis=0, concat_axis=0, tiled=...]
    concatenate x19 -> x0, other arithmetic: 11.6 us -> none  [with_halo(): block = jnp.concatenate([low, block, high], axis=dim)]
    add x17 -> x0, other arithmetic: 11.5 us -> none  [the longest x16 10.6 us: diffuse_once(): result = center + east_flux + west_flux + north_flux + south_flux]
    scatter x3 -> x0, local copies, waits for them, and re-layouts: 10.5 us -> none  [the longest x1 6.28 us: body(): weights_send = jnp.zeros((slot_total,) + obs_weights.shape[1:], jnp.bfloa...]
    slice x26 -> x0, local copies, waits for them, and re-layouts: 8.89 us -> none  [the longest x18 5.8 us: with_halo(): lax.slice_in_dim(block, block.shape[dim] - width, None, axis=dim)]
  transfers between devices with their start and end apart: 72 -> 0, of which waited for: 29 -> 0; matrix products, arithmetic and copies ran while one was open for 6% -> 0% of each run, Pallas kernels for 0% -> 0%
where the time goes in v1:
time: 88.5 us; the launch traced here: 88.3 us
  Pallas kernels  84.4 us (95%)
  local copies, waits for them, and re-layouts  3.19 us (4%)
    pallas_call x1, Pallas kernels, body(): pl.pallas_call(functools.partial(kernel, n_x, n_y), out_shape=(jax.ShapeD...  84.4 us
    unnamed x2, local copies, waits for them, and re-layouts  3.19 us

profile of v1, /device:TPU:1, one launch (start us, length us, event | category | flops | bytes accessed | tf_op | source)
XLA Modules:
  0.0 88.3 jit_solution(11577641609789112176)
XLA Ops:
  0.6 84.4 %variational_gradient.1 = (f32[4,128,256]{2,1,0:T(8,128)}, f32[32,128]{1,0:T(8,128)}) custom-call(f32[4,128,256]{2,1,0:T(8,128)} %control.1, f32[4,128,256]{2,1,0:T(8,128)} %background_std.1, f32[2,128,256]{2,1,0:T(8,128)} %kappa_x.1, f32[2,128,256]{2,1,0:T(8,128)} %kappa_y.1, s32[2,128,256]{2,1,0:T(8,128)} %sea_mask.1, bf16[32,128,256]{2,1,0:T(8,128)(2,1)} %obs_weights.1, ...), custom_call_target="tpu_custom_call" | custom-call | tf_op jit(solution)/shard_map/variational_gradient/pallas_call | solution.py:534
  85.1 1.9 %copy.14 = f32[4,128,256]{2,1,0:T(8,128)} copy(f32[4,128,256]{2,1,0:T(8,128)} %get-tuple-element.4) | data formatting | bytes 1048576
  86.9 1.3 %copy.15 = f32[32,128]{1,0:T(8,128)} copy(f32[32,128]{1,0:T(8,128)} %get-tuple-element.5) | data formatting | bytes 32768

commit v2 on v1

--- a/solution.py
+++ b/solution.py
@@ -39,41 +39,45 @@
     return [jnp.where(first_lane, rolled[(t - 1) % count], rolled[t]) for t in range(count)]
 
 
-def diffuse_step(src, dst, fx, fy, levels, rows):
-    ntile = src.shape[1]
+def diffuse(field, spare, fx, fy, levels, rows):
+    ntile = field.shape[1]
     first_lane = lane_iota((CHUNK, LANES)) == 0
     last_lane = lane_iota((CHUNK, LANES)) == LANES - 1
-    for level in range(levels):
-        for base in range(RIM, RIM + rows + 2 * RIM, CHUNK):
+
+    def sweep(src, dst):
+        def chunk(number, carry):
+            base = RIM + number * CHUNK
             here, above, below = (
-                pl.ds(base, CHUNK),
+                pl.ds(pl.multiple_of(base, 8), CHUNK),
                 pl.ds(base + 1, CHUNK),
                 pl.ds(base - 1, CHUNK),
             )
-            east = [fx[level, t, here, :] for t in range(ntile)]
-            west = [fx[level, t, below, :] for t in range(ntile)]
-            north = [fy[level, t, here, :] for t in range(ntile)]
-            for var in range(VARS):
-                plane = var * levels + level
-                center = [src[plane, t, here, :] for t in range(ntile)]
-                up = north_of(center, last_lane)
-                flux = [north[t] * (up[t] - center[t]) for t in range(ntile)]
-                back = south_of(flux, first_lane)
-                for t in range(ntile):
-                    cell = center[t]
-                    dst[plane, t, here, :] = (
-                        cell
-                        + east[t] * (src[plane, t, above, :] - cell)
-                        + west[t] * (src[plane, t, below, :] - cell)
-                        + flux[t]
-                        - back[t]
-                    )
-
-
-def diffuse(first, second, fx, fy, levels, rows):
+            for level in range(levels):
+                east = [fx[level, t, here, :] for t in range(ntile)]
+                west = [fx[level, t, below, :] for t in range(ntile)]
+                north = [fy[level, t, here, :] for t in range(ntile)]
+                for var in range(VARS):
+                    plane = var * levels + level
+                    center = [src[plane, t, here, :] for t in range(ntile)]
+                    up = north_of(center, last_lane)
+                    flux = [north[t] * (up[t] - center[t]) for t in range(ntile)]
+                    back = south_of(flux, first_lane)
+                    for t in range(ntile):
+                        cell = center[t]
+                        dst[plane, t, here, :] = (
+                            cell
+                            + east[t] * (src[plane, t, above, :] - cell)
+                            + west[t] * (src[plane, t, below, :] - cell)
+                            + flux[t]
+                            - back[t]
+                        )
+            return carry
+
+        lax.fori_loop(0, (rows + 2 * RIM) // CHUNK, chunk, 0)
+
     def twice(_, carry):
-        diffuse_step(first, second, fx, fy, levels, rows)
-        diffuse_step(second, first, fx, fy, levels, rows)
+        sweep(field, spare)
+        sweep(spare, field)
         return carry
 
     lax.fori_loop(0, NSTEP // 2, twice, 0)

time: 88.5 us -> 72.7 us (0.82)
  Pallas kernels: 84.4 us -> 68.6 us
    pallas_call x1, Pallas kernels: 84.4 us -> 68.6 us  [body(): pl.pallas_call(functools.partial(kernel, n_x, n_y), out_shape=(jax.ShapeD...]
where the time goes in v2:
time: 72.7 us; the launch traced here: 72.4 us
  Pallas kernels  68.6 us (94%)
  local copies, waits for them, and re-layouts  3.19 us (4%)
    pallas_call x1, Pallas kernels, body(): pl.pallas_call(functools.partial(kernel, n_x, n_y), out_shape=(jax.ShapeD...  68.6 us
    unnamed x2, local copies, waits for them, and re-layouts  3.19 us

profile of v2, /device:TPU:1, one launch (start us, length us, event | category | flops | bytes accessed | tf_op | source)
XLA Modules:
  0.0 72.4 jit_solution(10231340850498982890)
XLA Ops:
  0.6 68.6 %variational_gradient.1 = (f32[4,128,256]{2,1,0:T(8,128)}, f32[32,128]{1,0:T(8,128)}) custom-call(f32[4,128,256]{2,1,0:T(8,128)} %control.1, f32[4,128,256]{2,1,0:T(8,128)} %background_std.1, f32[2,128,256]{2,1,0:T(8,128)} %kappa_x.1, f32[2,128,256]{2,1,0:T(8,128)} %kappa_y.1, s32[2,128,256]{2,1,0:T(8,128)} %sea_mask.1, bf16[32,128,256]{2,1,0:T(8,128)(2,1)} %obs_weights.1, ...), custom_call_target="tpu_custom_call" | custom-call | tf_op jit(solution)/shard_map/variational_gradient/pallas_call | solution.py:538
  69.2 1.9 %copy.14 = f32[4,128,256]{2,1,0:T(8,128)} copy(f32[4,128,256]{2,1,0:T(8,128)} %get-tuple-element.4) | data formatting | bytes 1048576
  71.1 1.3 %copy.15 = f32[32,128]{1,0:T(8,128)} copy(f32[32,128]{1,0:T(8,128)} %get-tuple-element.5) | data formatting | bytes 32768

commit v3 on v1

--- a/solution.py
+++ b/solution.py
@@ -13,7 +13,7 @@
 RIM = 8
 CAP = 2
 TOP = 2 * RIM
-CHUNK = 16
+GROUP = 8
 MESH = pl.DeviceIdType.MESH
 F32 = jnp.float32
 BF16 = jnp.bfloat16
@@ -39,17 +39,15 @@
     return [jnp.where(first_lane, rolled[(t - 1) % count], rolled[t]) for t in range(count)]
 
 
-def diffuse_step(src, dst, fx, fy, levels, rows):
-    ntile = src.shape[1]
-    first_lane = lane_iota((CHUNK, LANES)) == 0
-    last_lane = lane_iota((CHUNK, LANES)) == LANES - 1
-    for level in range(levels):
-        for base in range(RIM, RIM + rows + 2 * RIM, CHUNK):
-            here, above, below = (
-                pl.ds(base, CHUNK),
-                pl.ds(base + 1, CHUNK),
-                pl.ds(base - 1, CHUNK),
-            )
+def diffuse(field, spare, fx, fy, levels, rows):
+    ntile = field.shape[1]
+    count = rows + 2 * RIM
+    here, above, below = pl.ds(RIM, count), pl.ds(RIM + 1, count), pl.ds(RIM - 1, count)
+    first_lane = lane_iota((count, LANES)) == 0
+    last_lane = lane_iota((count, LANES)) == LANES - 1
+
+    def sweep(src, dst):
+        for level in range(levels):
             east = [fx[level, t, here, :] for t in range(ntile)]
             west = [fx[level, t, below, :] for t in range(ntile)]
             north = [fy[level, t, here, :] for t in range(ntile)]
@@ -69,11 +67,9 @@
                         - back[t]
                     )
 
-
-def diffuse(first, second, fx, fy, levels, rows):
     def twice(_, carry):
-        diffuse_step(first, second, fx, fy, levels, rows)
-        diffuse_step(second, first, fx, fy, levels, rows)
+        sweep(field, spare)
+        sweep(spare, field)
         return carry
 
     lax.fori_loop(0, NSTEP // 2, twice, 0)
@@ -103,10 +99,10 @@
     kappa_y,
     sea_mask,
     obs_weights,
-    obs_values,
-    obs_rinv,
-    tile_row,
-    offset_row,
+    obs_values_in,
+    obs_rinv_in,
+    tile_row_in,
+    offset_row_in,
     gradient,
     departures,
     xin,
@@ -131,6 +127,10 @@
     term_in,
     terms,
     out_tile,
+    obs_values,
+    obs_rinv,
+    tile_row,
+    offset_row,
     load_sem,
     x_send,
     x_recv,
@@ -186,6 +186,11 @@
         load(kappa_y.at[:, :, span], xin.at[pl.ds(planes + levels, levels), t, own, :])
         load(control.at[:, :, span], xin.at[pl.ds(0, planes), t, own, :])
     late = len(loads)
+    load(tile_row_in, tile_row)
+    load(offset_row_in, offset_row)
+    small = len(loads)
+    load(obs_values_in, obs_values)
+    load(obs_rinv_in, obs_rinv)
     for t in range(segs):
         load(background_std.at[:, :, pl.ds(t * LANES, LANES)], std.at[:, t, :, :])
     load(obs_weights, weights)
@@ -201,6 +206,8 @@
             fx[level, t, pl.ds(0, RIM), :] = edge
             sea[level, t, pl.ds(height - RIM, RIM), :] = edge
 
+    for copy in loads[late:small]:
+        copy.wait()
     row = tile_row[...].astype(F32)
     pair = (blocks, blocks)
     diagonal = lane_iota(pair) == row_iota(pair)
@@ -370,7 +377,7 @@
 
     diffuse(field_a, field_b, fx, fy, levels, rows)
 
-    for copy in loads[late:]:
+    for copy in loads[small:]:
         copy.wait()
     sent_index.wait()
     asked = jnp.concatenate(
@@ -420,24 +427,46 @@
         [patches, jnp.zeros((LANES - blocks, patch_width), BF16)], axis=0
     )
 
-    def one_equivalent(b, total):
+    def some_equivalents(group, total):
+        first = group * GROUP
         product = lax.dot_general(
-            weights[b], padded, (((1,), (1,)), ((), ())), preferred_element_type=F32
+            weights[pl.ds(first, GROUP)].reshape(GROUP * nobs, patch_width),
+            padded,
+            (((1,), (1,)), ((), ())),
+            preferred_element_type=F32,
         )
-        return jnp.where(obs_lane == b, product, total)
-
-    equivalents = lax.fori_loop(0, blocks, one_equivalent, jnp.zeros((nobs, LANES), F32))
+        for number in range(GROUP):
+            total = jnp.where(
+                obs_lane == first + number, product[number * nobs : (number + 1) * nobs], total
+            )
+        return total
+
+    equivalents = lax.fori_loop(
+        0, blocks // GROUP, some_equivalents, jnp.zeros((nobs, LANES), F32)
+    )
     departed = obs_rinv[...] * (equivalents.T[:blocks] - obs_values[...])
     departures[...] = departed
     low = departed.astype(BF16).astype(F32)
     low_cols = jnp.concatenate([low, jnp.zeros((LANES - blocks, nobs), F32)], axis=0).T
 
-    def one_term(b, carry):
-        column = jnp.sum(jnp.where(obs_lane == b, low_cols, 0.0), axis=1, keepdims=True)
-        terms[pl.ds(b, 1), :] = jnp.sum(weights[b].astype(F32) * column, axis=0, keepdims=True)
+    def some_terms(group, carry):
+        first = group * GROUP
+        columns = [
+            jnp.sum(jnp.where(obs_lane == first + number, low_cols, 0.0), axis=1, keepdims=True)
+            for number in range(GROUP)
+        ]
+        terms[pl.ds(pl.multiple_of(first, GROUP), GROUP), :] = jnp.concatenate(
+            [
+                jnp.sum(
+                    weights[first + number].astype(F32) * columns[number], axis=0, keepdims=True
+                )
+                for number in range(GROUP)
+            ],
+            axis=0,
+        )
         return carry
 
-    lax.fori_loop(0, blocks, one_term, 0)
+    lax.fori_loop(0, blocks // GROUP, some_terms, 0)
     outgoing = exact_dot(slot_block.astype(BF16), terms[...])
     for c in range(CAP):
         term_out[:, 0, pl.ds(c * patch_width, patch_width)] = outgoing[c * n_x : (c + 1) * n_x]
@@ -469,6 +498,7 @@
                     std[plane, s]
                     * forcing[start : start + rows, v * LANES : (v + 1) * LANES]
                 )
+    sent_x2 = send_x((field_c,), (x2_send, x2_recv))
     for side, t in ((0, 0), (1, segs - 1)):
         strip = jnp.zeros((rows, LANES), F32)
         for plane in range(planes):
@@ -479,7 +509,6 @@
             here = (strip_lane >= plane * RIM) & (strip_lane < (plane + 1) * RIM)
             strip = jnp.where(here, value, strip)
         strip_out2[side] = strip
-    sent_x2 = send_x((field_c,), (x2_send, x2_recv))
     sent_y2 = send_y(strip_out2, strip_in2, (y2_send, y2_recv))
     for copy in sent_x2 + sent_y2:
         copy.wait()
@@ -491,10 +520,7 @@
     stores = []
     for s in range(segs):
         for plane in range(planes):
-            out_tile[plane, s] = (
-                xin[plane, s, own, :]
-                + sea[plane % levels, s, own, :] * field_c[plane, s, own, :]
-            )
+            out_tile[plane, s] = sea[plane % levels, s, own, :] * field_c[plane, s, own, :]
         copy = pltpu.make_async_copy(
             out_tile.at[:, s, :, :],
             gradient.at[:, :, pl.ds(s * LANES, LANES)],
@@ -504,6 +530,11 @@
         stores.append(copy)
     for copy in stores:
         copy.wait()
+
+
+def finish(increment, control, departed, gradient, departures):
+    gradient[...] = control[...] + increment[...]
+    departures[...] = departed[...]
 
 
 def body(
@@ -531,13 +562,13 @@
     dma = pltpu.SemaphoreType.DMA
     field = pltpu.VMEM((planes, segs + 1, height, LANES), F32)
     face = pltpu.VMEM((levels, segs + 1, height, LANES), F32)
-    return pl.pallas_call(
+    increment, departed = pl.pallas_call(
         functools.partial(kernel, n_x, n_y),
         out_shape=(
             jax.ShapeDtypeStruct(control.shape, F32),
             jax.ShapeDtypeStruct(obs_values.shape, F32),
         ),
-        in_specs=[hbm] * 6 + [vmem] * 4,
+        in_specs=[hbm] * 10,
         out_specs=(hbm, vmem),
         scratch_shapes=[
             pltpu.VMEM((inputs, segs, height, LANES), F32),
@@ -562,7 +593,11 @@
             pltpu.VMEM((n_x, 1, CAP * width), F32),
             pltpu.VMEM((blocks, width), F32),
             pltpu.VMEM((planes, segs, rows, LANES), F32),
-            dma((5 * segs + 1,)),
+            pltpu.VMEM((blocks, nobs), F32),
+            pltpu.VMEM((blocks, nobs), F32),
+            pltpu.VMEM((1, blocks), jnp.int32),
+            pltpu.VMEM((1, blocks), jnp.int32),
+            dma((5 * segs + 5,)),
             dma((4,)),
             dma((4,)),
             dma((6,)),
@@ -590,6 +625,19 @@
         obs_tile.reshape(1, blocks),
         obs_offset.reshape(1, blocks),
     )
+    slab = pl.BlockSpec((1, rows, cols), lambda plane: (plane, 0, 0))
+    whole = pl.BlockSpec((blocks, nobs), lambda plane: (0, 0))
+    return pl.pallas_call(
+        finish,
+        grid=(planes,),
+        out_shape=(
+            jax.ShapeDtypeStruct(control.shape, F32),
+            jax.ShapeDtypeStruct(obs_values.shape, F32),
+        ),
+        in_specs=[slab, slab, whole],
+        out_specs=(slab, whole),
+        name="add_control",
+    )(increment, control, departed)
 
 
 def solution(mesh):

time: 88.5 us -> 53.4 us (0.60)
  Pallas kernels: 84.4 us -> 52.6 us
  local copies, waits for them, and re-layouts: 3.19 us -> 0 us
    pallas_call x1, Pallas kernels: 84.4 us -> 49.3 us  [body(): pl.pallas_call(functools.partial(kernel, n_x, n_y), out_shape=(jax.ShapeD...]
    pallas_call x0 -> x1, Pallas kernels: none -> 3.33 us  [body(): pl.pallas_call(finish, grid=(planes,), out_shape=(jax.ShapeDtypeStruct(co...]
    unnamed x2 -> x0, local copies, waits for them, and re-layouts: 3.19 us -> none
where the time goes in v3:
time: 53.4 us; the launch traced here: 53.2 us
  Pallas kernels  52.6 us (99%)
  between operations  0.64 us (1%)
    pallas_call x1, Pallas kernels, body(): pl.pallas_call(functools.partial(kernel, n_x, n_y), out_shape=(jax.ShapeD...  49.3 us
    pallas_call x1, Pallas kernels, body(): pl.pallas_call(finish, grid=(planes,), out_shape=(jax.ShapeDtypeStruct(co...  3.33 us

profile of v3, /device:TPU:1, one launch (start us, length us, event | category | flops | bytes accessed | tf_op | source)
XLA Modules:
  0.0 53.2 jit_solution(7154456978508585616)
XLA Ops:
  0.6 49.3 %variational_gradient.1 = (f32[4,128,256]{2,1,0:T(8,128)}, f32[32,128]{1,0:T(8,128)}) custom-call(f32[4,128,256]{2,1,0:T(8,128)} %control.3, f32[4,128,256]{2,1,0:T(8,128)} %background_std.1, f32[2,128,256]{2,1,0:T(8,128)} %kappa_x.1, f32[2,128,256]{2,1,0:T(8,128)} %kappa_y.1, s32[2,128,256]{2,1,0:T(8,128)} %sea_mask.1, bf16[32,128,256]{2,1,0:T(8,128)(2,1)} %obs_weights.1, ...), custom_call_target="tpu_custom_call" | custom-call | tf_op jit(solution)/shard_map/variational_gradient/pallas_call | solution.py:565
  49.9 3.3 %add_control.1 = (f32[4,128,256]{2,1,0:T(8,128)}, f32[32,128]{1,0:T(8,128)}) custom-call(f32[4,128,256]{2,1,0:T(8,128)} %get-tuple-element.4.increment, f32[4,128,256]{2,1,0:T(8,128)} %control.3, f32[32,128]{1,0:T(8,128)} %get-tuple-element.5.departed), custom_call_target="tpu_custom_call" | custom-call | tf_op jit(solution)/shard_map/add_control/pallas_call | solution.py:630

commit v4 on v3

--- a/solution.py
+++ b/solution.py
@@ -14,6 +14,7 @@
 CAP = 2
 TOP = 2 * RIM
 GROUP = 8
+CHUNK = 48
 MESH = pl.DeviceIdType.MESH
 F32 = jnp.float32
 BF16 = jnp.bfloat16
@@ -39,33 +40,62 @@
     return [jnp.where(first_lane, rolled[(t - 1) % count], rolled[t]) for t in range(count)]
 
 
-def diffuse(field, spare, fx, fy, levels, rows):
-    ntile = field.shape[1]
-    count = rows + 2 * RIM
-    here, above, below = pl.ds(RIM, count), pl.ds(RIM + 1, count), pl.ds(RIM - 1, count)
-    first_lane = lane_iota((count, LANES)) == 0
-    last_lane = lane_iota((count, LANES)) == LANES - 1
+def to_lanes(nat, target, planes):
+    depth, height, _ = target.shape
+    run = height // depth
+    size = height - 2 * TOP
+    low_lane = lane_iota((RIM, LANES)) < LANES // 2
+    for step in range(depth):
+        pick = pl.ds(step, run, stride=depth)
+        own = jnp.concatenate(
+            [nat[plane, tile, pick, :] for tile in range(2) for plane in planes], axis=0
+        ).T
+        rim = jnp.concatenate([nat[plane, 2, pick, :] for plane in planes] * 2, axis=0).T
+        target[step, pl.ds(TOP, size), :] = own
+        target[step, pl.ds(RIM, RIM), :] = jnp.where(
+            low_lane, rim[size - RIM :], pltpu.roll(own[size - RIM :], LANES // 2, 1)
+        )
+        target[step, pl.ds(TOP + size, RIM), :] = jnp.where(
+            low_lane, pltpu.roll(own[:RIM], LANES // 2, 1), rim[:RIM]
+        )
+
+
+def from_lanes(source, nat, planes):
+    depth, height, _ = source.shape
+    run = height // depth
+    for step in range(depth):
+        pick = pl.ds(step, run, stride=depth)
+        rows = source[step, pl.ds(TOP, height - 2 * TOP), :].T
+        for tile in range(2):
+            for plane in range(planes):
+                start = (tile * planes + plane) * run
+                nat[plane, tile, pick, :] = rows[start : start + run]
+
+
+def diffuse(field, spare, fx, fy):
+    depth, height, _ = field.shape
 
     def sweep(src, dst):
-        for level in range(levels):
-            east = [fx[level, t, here, :] for t in range(ntile)]
-            west = [fx[level, t, below, :] for t in range(ntile)]
-            north = [fy[level, t, here, :] for t in range(ntile)]
-            for var in range(VARS):
-                plane = var * levels + level
-                center = [src[plane, t, here, :] for t in range(ntile)]
-                up = north_of(center, last_lane)
-                flux = [north[t] * (up[t] - center[t]) for t in range(ntile)]
-                back = south_of(flux, first_lane)
-                for t in range(ntile):
-                    cell = center[t]
-                    dst[plane, t, here, :] = (
-                        cell
-                        + east[t] * (src[plane, t, above, :] - cell)
-                        + west[t] * (src[plane, t, below, :] - cell)
-                        + flux[t]
-                        - back[t]
-                    )
+        for base in range(RIM, height - RIM, CHUNK):
+            here, above, below = pl.ds(base, CHUNK), pl.ds(base + 1, CHUNK), pl.ds(base - 1, CHUNK)
+            wrapped = pltpu.roll(src[0, here, :], LANES - 1, 1)
+            back = None
+            for step in range(depth):
+                cell = src[step, here, :]
+                east = src[step + 1, here, :] if step < depth - 1 else wrapped
+                flux = fx[step, here, :] * (east - cell)
+                total = (
+                    cell
+                    + flux
+                    + fy[step, here, :] * (src[step, above, :] - cell)
+                    + fy[step, below, :] * (src[step, below, :] - cell)
+                )
+                if step:
+                    dst[step, here, :] = total - back
+                else:
+                    dst[0, here, :] = total
+                back = flux
+            dst[0, here, :] = dst[0, here, :] - pltpu.roll(back, 1, 1)
 
     def twice(_, carry):
         sweep(field, spare)
@@ -113,8 +143,11 @@
     fx,
     fy,
     field_a,
-    field_b,
     field_c,
+    lane_a,
+    lane_b,
+    lane_x,
+    lane_y,
     strip_out,
     strip_in,
     strip_out2,
@@ -196,15 +229,22 @@
     load(obs_weights, weights)
 
     edge = jnp.zeros((RIM, LANES), F32)
-    for ref in (field_a, field_b, field_c):
+    for ref in (field_a, field_c):
         for plane in range(planes):
             for t in range(segs + 1):
                 ref[plane, t, pl.ds(0, RIM), :] = edge
                 ref[plane, t, pl.ds(height - RIM, RIM), :] = edge
     for level in range(levels):
         for t in range(segs + 1):
-            fx[level, t, pl.ds(0, RIM), :] = edge
+            for ref in (fx, fy):
+                ref[level, t, pl.ds(0, RIM), :] = edge
+                ref[level, t, pl.ds(height - RIM, RIM), :] = edge
             sea[level, t, pl.ds(height - RIM, RIM), :] = edge
+
+    for ref in (lane_a, lane_b, lane_x, lane_y):
+        for step in range(lane_a.shape[0]):
+            ref[step, pl.ds(0, RIM), :] = edge
+            ref[step, pl.ds(height - RIM, RIM), :] = edge
 
     for copy in loads[late:small]:
         copy.wait()
@@ -375,7 +415,12 @@
             )
             fy[level, t, ext, :] = fy[level, t, ext, :] * wet_north[t]
 
-    diffuse(field_a, field_b, fx, fy, levels, rows)
+    faces = list(range(levels)) * VARS
+    to_lanes(field_a, lane_a, range(planes))
+    to_lanes(fx, lane_x, faces)
+    to_lanes(fy, lane_y, faces)
+    diffuse(lane_a, lane_b, lane_x, lane_y)
+    from_lanes(lane_a, field_a, planes)
 
     for copy in loads[small:]:
         copy.wait()
@@ -515,7 +560,9 @@
     for plane in range(planes):
         field_c[plane, segs, ext, :] = unpack(strip_in2, plane)
 
-    diffuse(field_c, field_b, fx, fy, levels, rows)
+    to_lanes(field_c, lane_a, range(planes))
+    diffuse(lane_a, lane_b, lane_x, lane_y)
+    from_lanes(lane_a, field_c, planes)
 
     stores = []
     for s in range(segs):
@@ -561,6 +608,8 @@
     vmem = pl.BlockSpec(memory_space=pltpu.VMEM)
     dma = pltpu.SemaphoreType.DMA
     field = pltpu.VMEM((planes, segs + 1, height, LANES), F32)
+    depth = height * planes * segs // LANES
+    lanes = pltpu.VMEM((depth, height, LANES), F32)
     face = pltpu.VMEM((levels, segs + 1, height, LANES), F32)
     increment, departed = pl.pallas_call(
         functools.partial(kernel, n_x, n_y),
@@ -580,7 +629,10 @@
             face,
             field,
             field,
-            field,
+            lanes,
+            lanes,
+            lanes,
+            lanes,
             pltpu.VMEM((2, rows, LANES), F32),
             pltpu.VMEM((2, height, LANES), F32),
             pltpu.VMEM((2, rows, LANES), F32),

time: 53.4 us -> 51 us (0.955)
  Pallas kernels: 52.6 us -> 50.2 us
    pallas_call x1, Pallas kernels: 49.3 us -> 46.8 us  [body(): pl.pallas_call(functools.partial(kernel, n_x, n_y), out_shape=(jax.ShapeD...]
where the time goes in v4:
time: 51 us; the launch traced here: 50.8 us
  Pallas kernels  50.2 us (98%)
  between operations  0.64 us (1%)
    pallas_call x1, Pallas kernels, body(): pl.pallas_call(functools.partial(kernel, n_x, n_y), out_shape=(jax.ShapeD...  46.8 us
    pallas_call x1, Pallas kernels, body(): pl.pallas_call(finish, grid=(planes,), out_shape=(jax.ShapeDtypeStruct(co...  3.33 us

profile of v4, /device:TPU:1, one launch (start us, length us, event | category | flops | bytes accessed | tf_op | source)
XLA Modules:
  0.0 50.8 jit_solution(6261236024044980615)
XLA Ops:
  0.6 46.8 %variational_gradient.1 = (f32[4,128,256]{2,1,0:T(8,128)}, f32[32,128]{1,0:T(8,128)}) custom-call(f32[4,128,256]{2,1,0:T(8,128)} %control.3, f32[4,128,256]{2,1,0:T(8,128)} %background_std.1, f32[2,128,256]{2,1,0:T(8,128)} %kappa_x.1, f32[2,128,256]{2,1,0:T(8,128)} %kappa_y.1, s32[2,128,256]{2,1,0:T(8,128)} %sea_mask.1, bf16[32,128,256]{2,1,0:T(8,128)(2,1)} %obs_weights.1, ...), custom_call_target="tpu_custom_call" | custom-call | tf_op jit(solution)/shard_map/variational_gradient/pallas_call | solution.py:614
  47.5 3.3 %add_control.1 = (f32[4,128,256]{2,1,0:T(8,128)}, f32[32,128]{1,0:T(8,128)}) custom-call(f32[4,128,256]{2,1,0:T(8,128)} %get-tuple-element.4.increment, f32[4,128,256]{2,1,0:T(8,128)} %control.3, f32[32,128]{1,0:T(8,128)} %get-tuple-element.5.departed), custom_call_target="tpu_custom_call" | custom-call | tf_op jit(solution)/shard_map/add_control/pallas_call | solution.py:682
